TPU v7x, 128 devices: a whole 4x4x4 slice. The times are simulated.
128 devices in a mesh: mpo: 8 (over z, x_lo), sec: 16 (over y, x_hi, core).
Axes of the slice: x: 4 (x_hi: 2, x_lo: 2; x = x_hi * 2 + x_lo), y: 4, z: 4, core: 2. Of those that a mesh axis runs over, the one named last changes fastest.
Arguments:
- wavefunction: bfloat16 [2, 128, 512, 512], P(None, 'sec'), may hold values from -6 to 6
- left_env: bfloat16 [16, 128, 512, 512], P('mpo', 'sec'), may hold values from -0.25 to 0.25
- right_env: bfloat16 [16, 128, 512, 512], P('mpo', 'sec'), may hold values from -0.0625 to 0.0625
- block_dims: int32 [128], P('sec'), may hold values from 128 to 512, as said below
- mpo_shift: int32 [16], P('mpo'), may hold values from -1 to 1
Outputs:
- sigma_blocks: bfloat16 [2, 128, 512, 512], P(None, 'sec', 'mpo')
Inputs may be any that keep to these rules, and one draw needn't show every extreme that they name: `block_dims`: some block is full.
All inputs are finite; a program needn't handle non-finite values.
Results may differ from a plain program's by a relative error of at most 0.0049.
Values may be sent and summed in bfloat16 or wider, within the bound.
A program may use at most 192 MiB of HBM per device.

v0:
```python
import jax
import jax.numpy as jnp
from jax import lax
from jax.sharding import PartitionSpec as P


def shifted(block, axis, distance):
    devices = range(lax.axis_size(axis))
    route = [((i - distance) % len(devices), i) for i in devices]
    return lax.ppermute(block, axis, route)


def body(wavefunction, left_env, right_env, block_dims, mpo_shift):
    sec_count = lax.axis_size("sec")
    sec_index = lax.axis_index("sec")
    lower_raw = shifted(wavefunction, "sec", 1)
    upper_raw = shifted(wavefunction, "sec", -1)
    empty_block = jnp.zeros_like(wavefunction[:, :1])
    from_lower = jnp.where(
        sec_index == 0, jnp.concatenate([empty_block, lower_raw[:, :-1]], axis=1), lower_raw
    )
    from_upper = jnp.where(
        sec_index == sec_count - 1,
        jnp.concatenate([upper_raw[:, 1:], empty_block], axis=1),
        upper_raw,
    )
    variants = jnp.stack([from_upper, wavefunction, from_lower])
    left_parts = []
    for mpo_row in range(left_env.shape[0]):
        chosen = lax.dynamic_index_in_dim(variants, mpo_shift[mpo_row] + 1, 0, keepdims=False)
        left_parts.append(
            jnp.einsum(
                "sab,ksbc->ksac", left_env[mpo_row], chosen, preferred_element_type=jnp.float32
            ).astype(jnp.bfloat16)
        )
    accumulated = jnp.zeros(wavefunction.shape, jnp.float32)
    for mpo_row in range(left_env.shape[0]):
        accumulated = accumulated + jnp.einsum(
            "ksac,scd->ksad",
            left_parts[mpo_row],
            right_env[mpo_row],
            preferred_element_type=jnp.float32,
        )
    summed = lax.psum_scatter(accumulated, "mpo", scatter_dimension=2, tiled=True)
    slab_rows = summed.shape[2]
    row_index = lax.axis_index("mpo") * slab_rows + jnp.arange(slab_rows, dtype=jnp.int32)
    col_index = jnp.arange(summed.shape[3], dtype=jnp.int32)
    block_limit = block_dims[None, :, None, None]
    inside = (row_index[None, None, :, None] < block_limit) & (
        col_index[None, None, None, :] < block_limit
    )
    return jnp.where(inside, summed, jnp.zeros_like(summed)).astype(jnp.bfloat16)


def solution(mesh):
    placed = (
        P(None, "sec", None, None),
        P("mpo", "sec", None, None),
        P("mpo", "sec", None, None),
        P("sec"),
        P("mpo"),
    )
    return jax.shard_map(
        body, mesh=mesh, in_specs=placed, out_specs=P(None, "sec", "mpo", None), check_vma=False
    )
```

profile of v0, /device:TPU:0, one launch (start us, length us, event | category | flops | bytes accessed | tf_op | source)
XLA Modules:
  0.0 626.2 jit_solution(14893305319358111210)
XLA Ops:
  6.5 0.0 reduce-scatter.2.cloned.1.call-start
  6.5 5.0 collective-permute-start
  11.6 0.0 collective-permute-start.1
  11.6 1.3 fusion.32
  15.3 175.0 %collective-permute-done = bf16[2,8,512,512]{3,2,1,0:T(8,128)(2,1)} collective-permute-done((bf16[2,8,512,512]{3,2,1,0:T(8,128)(2,1)}, bf16[2,8,512,512]{3,2,1,0:T(8,128)(2,1)}, u32[]{:S(2)}, u32[]{:S(2)}) %collective-permute-start) | collective-permute-done | bytes 8388640 | tf_op jit(solution)/shard_map/ppermute | solution.py:10
  190.3 3.6 slice.32
  193.9 0.0 collective-permute-done.1
  193.9 6.6 %slice.33 = bf16[2,7,512,512]{3,2,1,0:T(8,128)(2,1)} slice(bf16[2,8,512,512]{3,2,1,0:T(8,128)(2,1)} %collective-permute-done.1), slice={[0:2], [0:7], [0:512], [0:512]} | slice | bytes 14680064 | tf_op jit(solution)/shard_map/slice | solution.py:20
  200.5 0.0 copy-start
  200.5 7.6 %select_bitcast_fusion.1 = bf16[1,2,8,512,512]{4,3,2,1,0:T(8,128)(2,1)} fusion(bf16[2,8,512,512]{3,2,1,0:T(8,128)(2,1)} %collective-permute-done, bf16[2,7,512,512]{3,2,1,0:T(8,128)(2,1)S(1)} %slice.32, pred[]{:T(512)S(6)} %eq.6), kind=kLoop, calls=%fused_computation.15 | loop fusion | flops 4194304 | bytes 24117248 | tf_op jit(solution)/shard_map/stack | solution.py:27
  208.1 1.0 copy-done
  209.1 3.9 select_bitcast_fusion
  213.0 17.6 %pad_maximum_fusion = bf16[3,2,8,512,512]{4,3,2,1,0:T(8,128)(2,1)} fusion(bf16[1,2,8,512,512]{4,3,2,1,0:T(8,128)(2,1)} %select_bitcast_fusion, bf16[1,2,8,512,512]{4,3,2,1,0:T(8,128)(2,1)} %bitcast.49, bf16[1,2,8,512,512]{4,3,2,1,0:T(8,128)(2,1)} %select_bitcast_fusion.1), kind=kLoop, calls=%fused_computation | loop fusion | flops 25165824 | bytes 50331648 | tf_op jit(solution)/shard_map/stack | solution.py:27
  230.6 12.5 %dynamic-slice_bitcast_fusion = (bf16[2,8,512,512]{3,2,1,0:T(8,128)(2,1)}, bf16[2,8,512,512]{3,2,1,0:T(8,128)(2,1)}) fusion(bf16[3,2,8,512,512]{4,3,2,1,0:T(8,128)(2,1)} %pad_maximum_fusion, s32[]{:T(128)S(6)} %select_n.30, s32[]{:T(128)S(6)} %select_n.29), kind=kLoop, calls=%fused_computation.11 | loop fusion | bytes 33554440 | tf_op jit(solution)/shard_map/jit(dynamic_index_in_dim)/squeeze | solution.py:30
  243.0 15.7 %fusion.4 = f32[8,2,512,512]{3,2,1,0:T(8,128)} fusion(bf16[2,8,512,512]{3,2,1,0:T(8,128)(2,1)} %get-tuple-element.6, bf16[2,8,512,512]{3,2,1,0:T(8,128)(2,1)} %param.7, bf16[2,8,512,512]{3,2,1,0:T(8,128)(2,1)} %param.6), kind=kOutput, calls=%fused_computation.4 | convolution fusion | flops 8594128896 | bytes 33554432 | tf_op jit(solution)/shard_map/ksac,scd->ksad/dot_general | solution.py:38
  258.7 24.1 %add_bitcast_fusion = f32[2,8,512,512]{3,2,0,1:T(8,128)} fusion(f32[8,2,512,512]{3,2,1,0:T(8,128)} %fusion.4, bf16[2,8,512,512]{3,2,1,0:T(8,128)(2,1)} %get-tuple-element.5, bf16[2,8,512,512]{3,2,1,0:T(8,128)(2,1)} %param.7, bf16[2,8,512,512]{3,2,1,0:T(8,128)(2,1)} %param.6), kind=kOutput, calls=%fused_computation.1 | convolution fusion | flops 8598323200 | bytes 50331648 | tf_op jit(solution)/shard_map/ksac,scd->ksad/dot_general | solution.py:38
  282.8 0.0 reduce-scatter.2.cloned.1.call-update
  282.9 0.6 copy-done.1
  283.5 0.1 broadcast_compare_fusion
  283.5 0.1 iota_compare_fusion
  283.6 0.2 broadcast_and_fusion
  283.8 332.5 %reduce-scatter.2.cloned.1.call-done = f32[2,8,64,512]{3,2,0,1:T(8,128)} async-done(((f32[2,8,512,512]{3,2,0,1:T(8,128)}), f32[2,8,64,512]{3,2,0,1:T(8,128)}) %reduce-scatter.2.cloned.1.call-update) | async-done | bytes 2097168 | tf_op jit(solution)/shard_map/reduce_scatter | solution.py:44
  616.4 1.9 select_convert_fusion
  618.3 1.1 copy.6
  (2 shorter events, 0.0 us)
Async XLA Ops:
  6.5 609.8 %reduce-scatter.2.cloned.1.call-start = ((), (), s32[]{:S(2)}) async-start(), calls=%async_computation.1 | async-start | bytes 18874368 | tf_op jit(solution)/shard_map/reduce_scatter | solution.py:44
  6.5 183.7 %collective-permute-start = (bf16[2,8,512,512]{3,2,1,0:T(8,128)(2,1)}, bf16[2,8,512,512]{3,2,1,0:T(8,128)(2,1)}, u32[]{:S(2)}, u32[]{:S(2)}) collective-permute-start(bf16[2,8,512,512]{3,2,1,0:T(8,128)(2,1)} %param.5), channel_id=1, source_target_pairs={{1,0},{2,1},{3,2},{4,3},{5,4},{6,5},{7,6},{8,7},{9,8},{10,9},{11,1... | collective-permute-start | bytes 25165832 | tf_op jit(solution)/shard_map/ppermute | solution.py:10
  11.6 182.3 %collective-permute-start.1 = (bf16[2,8,512,512]{3,2,1,0:T(8,128)(2,1)}, bf16[2,8,512,512]{3,2,1,0:T(8,128)(2,1)}, u32[]{:S(2)}, u32[]{:S(2)}) collective-permute-start(bf16[2,8,512,512]{3,2,1,0:T(8,128)(2,1)} %param.5), channel_id=1, source_target_pairs={{15,0},{0,1},{1,2},{2,3},{3,4},{4,5},{5,6},{6,7},{7,8},{8,9},{9,10... | collective-permute-start | bytes 25165832 | tf_op jit(solution)/shard_map/ppermute | solution.py:10
  200.5 8.6 %copy-start = (bf16[2,7,512,512]{3,2,1,0:T(8,128)(2,1)S(1)}, bf16[2,7,512,512]{3,2,1,0:T(8,128)(2,1)}, u32[]{:S(2)}) copy-start(bf16[2,7,512,512]{3,2,1,0:T(8,128)(2,1)} %slice.33) | copy-start | bytes 22020100
  282.8 0.7 copy-start.1
Sparse Core Ops, SparseCore 0:
  283.0 333.3 reduce-scatter.1
where the time goes:
time: 627 us; the launch traced here: 626 us
  waiting for transfers between devices  508 us (81%)
  matrix products  39.8 us (6%)
  other arithmetic  31.3 us (5%)
  local copies, waits for them, and re-layouts  26.7 us (4%)
  between operations  15.9 us (3%)
    reduce_scatter x1, waiting for transfers between devices, body(): lax.psum_scatter(accumulated, 'mpo', scatter_dimension=2, tiled=True)  333 us
    ppermute x2, waiting for transfers between devices, shifted(): return lax.ppermute(block, axis, route)  175 us
    dot_general x2, matrix products, body(): jnp.einsum('ksac,scd->ksad', left_parts[mpo_row], right_env[mpo_row], pre...  39.8 us
    another operation x3, other arithmetic, body(): variants = jnp.stack([from_upper, wavefunction, from_lower])  29.1 us
  transfers between devices with their start and end apart: 3, of which 2 were waited for; matrix products, arithmetic and copies ran while one was open for 1% of the time, Pallas kernels for 0%

commit v1 on v0

v1 whole, which is shorter than its diff:
```python
import functools

import jax
import jax.numpy as jnp
from jax import lax
from jax.experimental import pallas as pl
from jax.experimental.pallas import tpu as pltpu
from jax.sharding import PartitionSpec as P

MESH = pl.DeviceIdType.MESH
RING = 4
ENV_RING = 4
CHIP, SIDE, FWD_UP, FWD_DOWN, PAIR, RELAY_UP, RELAY_DOWN, SUM_UP, SUM_DOWN = range(9)
KINDS = 9


def kernel(
    shift_ref, dims_ref, wave_ref, left_ref, right_ref, out_ref,
    own, chip, side, left_buf, right_buf, chosen, parts, pair_send, pair_recv, total,
    relay_send, relay_recv, sum_send, sum_recv,
    send_sem, recv_sem, own_sem, left_sem, right_sem,
):
    slots, block = wave_ref.shape[1], wave_ref.shape[2]
    half = block // 2
    slab = block // 8
    mpo = lax.axis_index("mpo")
    sec = lax.axis_index("sec")
    secs = lax.axis_size("sec")
    core = sec % 2
    z = mpo // 2
    x_lo = mpo % 2
    k_side = z % 2
    up = ((mpo + 2) % 8, sec)
    down = ((mpo + 6) % 8, sec)
    pair = (mpo + 1 - 2 * x_lo, sec)
    chip_mate = (mpo, sec + 1 - 2 * core)
    side_mate = (mpo + 1 - 2 * x_lo, (sec + secs - 1 + 2 * core) % secs)
    first = (secs - 1 - sec) // (secs - 1)
    last = sec // (secs - 1)

    def remote(kind, slot, src, dst, device):
        return pltpu.make_async_remote_copy(
            src_ref=src, dst_ref=dst, send_sem=send_sem.at[kind, slot],
            recv_sem=recv_sem.at[kind, slot], device_id=device, device_id_type=MESH,
        )

    def chip_copy(slot):
        return remote(CHIP, slot, wave_ref.at[:, slot], chip.at[slot], chip_mate)

    def side_copy(slot):
        source = (slot + first - last + slots) % slots
        return remote(SIDE, slot, wave_ref.at[k_side, source], side.at[slot, k_side], side_mate)

    def forward_up(slot, k):
        piece = side.at[slot, k, pl.ds(0, half)]
        return remote(FWD_UP, slot, piece, piece, up)

    def forward_down(slot, k):
        piece = side.at[slot, k, pl.ds(half, half)]
        return remote(FWD_DOWN, slot, piece, piece, down)

    def pair_copy(slot):
        return remote(PAIR, slot, pair_send.at[slot], pair_recv.at[slot], pair)

    def relay_copy(way, slot):
        return remote(RELAY_UP + way, slot, relay_send.at[way, slot], relay_recv.at[way, slot], (up, down)[way])

    def sum_copy(way, slot):
        return remote(SUM_UP + way, slot, sum_send.at[way, slot], sum_recv.at[way, slot], (up, down)[way])

    def own_copy(slot):
        return pltpu.make_async_copy(wave_ref.at[:, slot], own.at[slot], own_sem.at[slot])

    def left_copy(slot):
        at = slot % ENV_RING
        return pltpu.make_async_copy(left_ref.at[:, slot], left_buf.at[at], left_sem.at[at])

    def right_copy(slot):
        at = slot % ENV_RING
        return pltpu.make_async_copy(right_ref.at[:, slot], right_buf.at[at], right_sem.at[at])

    barrier = pltpu.get_barrier_semaphore()
    for mate in (up, down, pair, chip_mate, side_mate):
        pl.semaphore_signal(barrier, inc=1, device_id=mate, device_id_type=MESH)

    def start_local(slot, carry):
        own_copy(slot).start()
        left_copy(slot).start()
        right_copy(slot).start()
        return carry

    lax.fori_loop(0, ENV_RING - 1, start_local, 0)
    pl.semaphore_wait(barrier, 5)

    def start_remote(slot, carry):
        side_copy(slot).start()
        chip_copy(slot).start()
        return carry

    lax.fori_loop(0, slots, start_remote, 0)

    def stage_forward(slot):
        side_copy(slot).wait_recv()
        forward_up(slot, k_side).start()
        forward_down(slot, k_side).start()

    def stage_finish(slot):
        sum_copy(0, slot).wait_recv()
        sum_copy(1, slot).wait_recv()
        limit = dims_ref[slot]
        shape = (2, slab, block)
        rows = mpo * slab + lax.broadcasted_iota(jnp.int32, shape, 1)
        cols = lax.broadcasted_iota(jnp.int32, shape, 2)
        value = total[slot % RING, z] + sum_recv[0, slot].astype(jnp.float32)
        value = value + sum_recv[1, slot].astype(jnp.float32)
        inside = (rows < limit) & (cols < limit)
        out_ref[:, slot] = jnp.where(inside, value, jnp.zeros_like(value)).astype(jnp.bfloat16)

    def stage_sum(slot):
        relay_copy(0, slot).wait_recv()
        relay_copy(1, slot).wait_recv()
        at = slot % RING
        above, below = (z + 1) % 4, (z + 3) % 4
        sum_send[0, slot, 0] = (total[at, above, 0] + relay_recv[0, slot].astype(jnp.float32)).astype(jnp.bfloat16)
        sum_send[0, slot, 1] = total[at, above, 1].astype(jnp.bfloat16)
        sum_send[1, slot, 0] = total[at, below, 0].astype(jnp.bfloat16)
        sum_send[1, slot, 1] = (total[at, below, 1] + relay_recv[1, slot].astype(jnp.float32)).astype(jnp.bfloat16)
        sum_copy(0, slot).start()
        sum_copy(1, slot).start()

    def stage_pair(slot):
        pair_copy(slot).wait_recv()
        at = slot % RING
        total[at] = total[at] + pair_recv[slot].astype(jnp.float32)
        far = (z + 2) % 4
        relay_send[0, slot] = total[at, far, 0].astype(jnp.bfloat16)
        relay_send[1, slot] = total[at, far, 1].astype(jnp.bfloat16)
        relay_copy(0, slot).start()
        relay_copy(1, slot).start()

    def stage_compute(slot):
        at = slot % ENV_RING
        own_copy(slot).wait()
        left_copy(slot).wait()
        right_copy(slot).wait()
        chip_copy(slot).wait_recv()
        forward_up(slot, 1 - k_side).wait_recv()
        forward_down(slot, 1 - k_side).wait_recv()
        missing = first * ((slots - 1 - slot) // (slots - 1)) + last * (slot // (slots - 1))
        for w in range(2):
            turn = shift_ref[w] * (1 - 2 * core)
            use_side = (turn == 1).astype(jnp.float32) * (1 - missing).astype(jnp.float32)
            use_chip = (turn == -1).astype(jnp.float32)
            use_own = (turn == 0).astype(jnp.float32)
            for k in range(2):
                chosen[k] = (
                    own[slot, k] * use_own.astype(jnp.bfloat16)
                    + chip[slot, k] * use_chip.astype(jnp.bfloat16)
                    + side[slot, k] * use_side.astype(jnp.bfloat16)
                )
            theirs = left_buf[at, w, :, 1 - x_lo].reshape(half, block)
            mine = left_buf[at, w, :, x_lo].reshape(half, block)
            rows = jnp.concatenate([theirs, mine], axis=0)
            for k in range(2):
                parts[k, w] = jnp.dot(rows, chosen[k], preferred_element_type=jnp.float32).astype(jnp.bfloat16)
        for k in range(2):
            both = jnp.dot(parts[k, 0], right_buf[at, 0], preferred_element_type=jnp.float32) + jnp.dot(
                parts[k, 1], right_buf[at, 1], preferred_element_type=jnp.float32
            )
            pair_send[slot, :, k] = both[:half].astype(jnp.bfloat16).reshape(4, slab, block)
            total[slot % RING, :, k] = both[half:].reshape(4, slab, block)
        pair_copy(slot).start()

    def step(i, carry):
        @pl.when(i < slots)
        def _():
            stage_forward(i)

        @pl.when(i + ENV_RING - 1 < slots)
        def _():
            start_local(i + ENV_RING - 1, 0)

        @pl.when(i >= 3)
        def _():
            stage_finish(i - 3)

        @pl.when((i >= 2) & (i < slots + 2))
        def _():
            stage_sum(i - 2)

        @pl.when((i >= 1) & (i < slots + 1))
        def _():
            stage_pair(i - 1)

        @pl.when(i < slots)
        def _():
            stage_compute(i)

        return carry

    lax.fori_loop(0, slots + 3, step, 0)

    def drain(slot, carry):
        side_copy(slot).wait_send()
        chip_copy(slot).wait_send()
        forward_up(slot, k_side).wait_send()
        forward_down(slot, k_side).wait_send()
        pair_copy(slot).wait_send()
        for way in range(2):
            relay_copy(way, slot).wait_send()
            sum_copy(way, slot).wait_send()
        return carry

    lax.fori_loop(0, slots, drain, 0)


def body(wavefunction, left_env, right_env, block_dims, mpo_shift):
    vectors, slots, block, _ = wavefunction.shape
    slab = block // 8
    left_env = left_env.reshape(2, slots, 4, 2, slab, block)
    bf16, f32 = jnp.bfloat16, jnp.float32
    smem = pl.BlockSpec(memory_space=pltpu.SMEM)
    anywhere = pl.BlockSpec(memory_space=pl.ANY)
    return pl.pallas_call(
        kernel,
        out_shape=jax.ShapeDtypeStruct((vectors, slots, slab, block), bf16),
        in_specs=[smem, smem, anywhere, anywhere, anywhere],
        out_specs=pl.BlockSpec(memory_space=pltpu.VMEM),
        scratch_shapes=[
            pltpu.VMEM((slots, 2, block, block), bf16),
            pltpu.VMEM((slots, 2, block, block), bf16),
            pltpu.VMEM((slots, 2, block, block), bf16),
            pltpu.VMEM((ENV_RING, 2, 4, 2, slab, block), bf16),
            pltpu.VMEM((ENV_RING, 2, block, block), bf16),
            pltpu.VMEM((2, block, block), bf16),
            pltpu.VMEM((2, 2, block, block), bf16),
            pltpu.VMEM((slots, 4, 2, slab, block), bf16),
            pltpu.VMEM((slots, 4, 2, slab, block), bf16),
            pltpu.VMEM((RING, 4, 2, slab, block), f32),
            pltpu.VMEM((2, slots, slab, block), bf16),
            pltpu.VMEM((2, slots, slab, block), bf16),
            pltpu.VMEM((2, slots, 2, slab, block), bf16),
            pltpu.VMEM((2, slots, 2, slab, block), bf16),
            pltpu.SemaphoreType.DMA((KINDS, slots)),
            pltpu.SemaphoreType.DMA((KINDS, slots)),
            pltpu.SemaphoreType.DMA((slots,)),
            pltpu.SemaphoreType.DMA((ENV_RING,)),
            pltpu.SemaphoreType.DMA((ENV_RING,)),
        ],
        compiler_params=pltpu.CompilerParams(
            collective_id=0, has_side_effects=True, vmem_limit_bytes=66 * 1000 * 1000
        ),
        name="matvec",
    )(mpo_shift, block_dims, wavefunction, left_env, right_env)


def solution(mesh):
    placed = (
        P(None, "sec", None, None),
        P("mpo", "sec", None, None),
        P("mpo", "sec", None, None),
        P("sec"),
        P("mpo"),
    )
    return jax.shard_map(
        body, mesh=mesh, in_specs=placed, out_specs=P(None, "sec", "mpo", None), check_vma=False
    )
```

time: 627 us -> 159 us (0.25)
  the two profiles are of different devices: /device:TPU:0 before, /device:TPU:30 now
where the time goes in v1:
time: 159 us
  Pallas kernels  156 us (98%)
  local copies, waits for them, and re-layouts  2.29 us (1%)
    pallas_call x1, Pallas kernels, body(): pl.pallas_call(kernel, out_shape=jax.ShapeDtypeStruct((vectors, slots, sl...  156 us

profile of v1, /device:TPU:30, one launch (start us, length us, event | category | flops | bytes accessed | tf_op | source)
XLA Modules:
  0.0 158.7 jit_solution(13431180564954575227)
XLA Ops:
  0.0 156.4 %matvec.1 = bf16[2,8,64,512]{3,2,1,0:T(8,128)(2,1)} custom-call(s32[2]{0:T(128)} %shift_ref.1, s32[8]{0:T(128)} %dims_ref.1, bf16[2,8,512,512]{3,2,1,0:T(8,128)(2,1)} %wave_ref.1, bf16[2,8,4,2,64,512]{5,4,3,2,1,0:T(8,128)(2,1)} %bitcast.1, bf16[2,8,512,512]{3,2,1,0:T(8,128)(2,1)} %right_ref.1), custom_call_target="tpu_custom_call" | custom-call | tf_op jit(solution)/shard_map/matvec/pallas_call | solution.py:224
  156.4 2.3 %copy.7 = bf16[2,8,64,512]{3,2,1,0:T(8,128)(2,1)} copy(bf16[2,8,64,512]{3,2,1,0:T(8,128)(2,1)} %matvec.1) | data formatting | bytes 2097152

commit v2 on v1

v2 whole, which is shorter than its diff:
```python
import functools

import jax
import jax.numpy as jnp
from jax import lax
from jax.experimental import pallas as pl
from jax.experimental.pallas import tpu as pltpu
from jax.sharding import PartitionSpec as P

MESH = pl.DeviceIdType.MESH
LAG = 2
RING = LAG + 3
ENV_RING = 4
CHIP, SIDE, FWD_UP, FWD_DOWN, PAIR, RELAY_UP, RELAY_DOWN, SUM_UP, SUM_DOWN = range(9)
KINDS = 9


def kernel(
    shift_ref, dims_ref, wave_ref, left_ref, right_ref, out_ref,
    own, chip, side, left_buf, right_buf, chosen, parts, pair_send, pair_recv, total,
    relay_send, relay_recv, sum_send, sum_recv,
    send_sem, recv_sem, own_sem, left_sem, right_sem,
):
    slots, block = wave_ref.shape[1], wave_ref.shape[2]
    units = 2 * slots
    half = block // 2
    quarter = block // 4
    slab = block // 8
    mpo = lax.axis_index("mpo")
    sec = lax.axis_index("sec")
    secs = lax.axis_size("sec")
    core = sec % 2
    z = mpo // 2
    x_lo = mpo % 2
    direct = (z % 2) * half
    indirect = half - direct
    up = ((mpo + 2) % 8, sec)
    down = ((mpo + 6) % 8, sec)
    pair = (mpo + 1 - 2 * x_lo, sec)
    chip_mate = (mpo, sec + 1 - 2 * core)
    side_mate = (mpo + 1 - 2 * x_lo, (sec + secs - 1 + 2 * core) % secs)
    first = (secs - 1 - sec) // (secs - 1)
    last = sec // (secs - 1)

    def remote(kind, unit, src, dst, device):
        return pltpu.make_async_remote_copy(
            src_ref=src, dst_ref=dst, send_sem=send_sem.at[kind, unit],
            recv_sem=recv_sem.at[kind, unit], device_id=device, device_id_type=MESH,
        )

    def chip_copy(unit):
        return remote(CHIP, unit, wave_ref.at[unit % 2, unit // 2], chip.at[unit], chip_mate)

    def side_copy(unit):
        source = (unit // 2 + first - last + slots) % slots
        rows = pl.ds(direct, half)
        return remote(SIDE, unit, wave_ref.at[unit % 2, source, rows], side.at[unit, rows], side_mate)

    def forward_up(unit, start):
        piece = side.at[unit, pl.ds(start, quarter)]
        return remote(FWD_UP, unit, piece, piece, up)

    def forward_down(unit, start):
        piece = side.at[unit, pl.ds(start + quarter, quarter)]
        return remote(FWD_DOWN, unit, piece, piece, down)

    def pair_copy(unit):
        return remote(PAIR, unit, pair_send.at[unit], pair_recv.at[unit], pair)

    def relay_copy(way, unit):
        return remote(RELAY_UP + way, unit, relay_send.at[way, unit], relay_recv.at[way, unit], (up, down)[way])

    def sum_copy(way, unit):
        return remote(SUM_UP + way, unit, sum_send.at[way, unit], sum_recv.at[way, unit], (up, down)[way])

    def own_copy(unit):
        return pltpu.make_async_copy(wave_ref.at[unit % 2, unit // 2], own.at[unit], own_sem.at[unit])

    def left_copy(slot):
        at = slot % ENV_RING
        return pltpu.make_async_copy(left_ref.at[:, slot], left_buf.at[at], left_sem.at[at])

    def right_copy(slot):
        at = slot % ENV_RING
        return pltpu.make_async_copy(right_ref.at[:, slot], right_buf.at[at], right_sem.at[at])

    barrier = pltpu.get_barrier_semaphore()
    for mate in (up, down, pair, chip_mate, side_mate):
        pl.semaphore_signal(barrier, inc=1, device_id=mate, device_id_type=MESH)

    def start_local(slot, carry):
        own_copy(2 * slot).start()
        own_copy(2 * slot + 1).start()
        left_copy(slot).start()
        right_copy(slot).start()
        return carry

    lax.fori_loop(0, ENV_RING - 1, start_local, 0)
    pl.semaphore_wait(barrier, 5)

    def start_remote(unit, carry):
        side_copy(unit).start()
        chip_copy(unit).start()
        return carry

    lax.fori_loop(0, units, start_remote, 0)

    def stage_forward(unit):
        side_copy(unit).wait_recv()
        forward_up(unit, direct).start()
        forward_down(unit, direct).start()

    def stage_finish(unit):
        sum_copy(0, unit).wait_recv()
        sum_copy(1, unit).wait_recv()
        limit = dims_ref[unit // 2]
        shape = (slab, block)
        rows = mpo * slab + lax.broadcasted_iota(jnp.int32, shape, 0)
        cols = lax.broadcasted_iota(jnp.int32, shape, 1)
        value = total[unit % RING, z] + sum_recv[0, unit].astype(jnp.float32)
        value = value + sum_recv[1, unit].astype(jnp.float32)
        inside = (rows < limit) & (cols < limit)
        out_ref[unit % 2, unit // 2] = jnp.where(inside, value, jnp.zeros_like(value)).astype(jnp.bfloat16)

    top, bottom = pl.ds(0, slab // 2), pl.ds(slab // 2, slab // 2)

    def stage_sum(unit):
        relay_copy(0, unit).wait_recv()
        relay_copy(1, unit).wait_recv()
        at = unit % RING
        above, below = (z + 1) % 4, (z + 3) % 4
        sum_send[0, unit, top] = (total[at, above, top] + relay_recv[0, unit].astype(jnp.float32)).astype(jnp.bfloat16)
        sum_send[0, unit, bottom] = total[at, above, bottom].astype(jnp.bfloat16)
        sum_send[1, unit, top] = total[at, below, top].astype(jnp.bfloat16)
        sum_send[1, unit, bottom] = (total[at, below, bottom] + relay_recv[1, unit].astype(jnp.float32)).astype(
            jnp.bfloat16
        )
        sum_copy(0, unit).start()
        sum_copy(1, unit).start()

    def stage_pair(unit):
        pair_copy(unit).wait_recv()
        at = unit % RING
        total[at] = total[at] + pair_recv[unit].astype(jnp.float32)
        far = (z + 2) % 4
        relay_send[0, unit] = total[at, far, top].astype(jnp.bfloat16)
        relay_send[1, unit] = total[at, far, bottom].astype(jnp.bfloat16)
        relay_copy(0, unit).start()
        relay_copy(1, unit).start()

    def stage_compute(unit):
        slot = unit // 2
        at = slot % ENV_RING
        own_copy(unit).wait()

        @pl.when(unit % 2 == 0)
        def _():
            left_copy(slot).wait()
            right_copy(slot).wait()

        chip_copy(unit).wait_recv()
        forward_up(unit, indirect).wait_recv()
        forward_down(unit, indirect).wait_recv()
        missing = first * ((slots - 1 - slot) // (slots - 1)) + last * (slot // (slots - 1))
        for w in range(2):
            turn = shift_ref[w] * (1 - 2 * core)
            use_side = (turn == 1).astype(jnp.float32) * (1 - missing).astype(jnp.float32)
            use_chip = (turn == -1).astype(jnp.float32)
            use_own = (turn == 0).astype(jnp.float32)
            chosen[w] = (
                own[unit] * use_own.astype(jnp.bfloat16)
                + chip[unit] * use_chip.astype(jnp.bfloat16)
                + side[unit] * use_side.astype(jnp.bfloat16)
            )
            theirs = left_buf[at, w, :, 1 - x_lo].reshape(half, block)
            mine = left_buf[at, w, :, x_lo].reshape(half, block)
            rows = jnp.concatenate([theirs, mine], axis=0)
            parts[w] = jnp.dot(rows, chosen[w], preferred_element_type=jnp.float32).astype(jnp.bfloat16)
        both = jnp.dot(parts[0], right_buf[at, 0], preferred_element_type=jnp.float32) + jnp.dot(
            parts[1], right_buf[at, 1], preferred_element_type=jnp.float32
        )
        pair_send[unit] = both[:half].astype(jnp.bfloat16).reshape(4, slab, block)
        total[unit % RING] = both[half:].reshape(4, slab, block)
        pair_copy(unit).start()

    def step(i, carry):
        @pl.when(i < units)
        def _():
            stage_forward(i)

        ahead = i // 2 + ENV_RING - 1

        @pl.when((i % 2 == 0) & (ahead < slots))
        def _():
            start_local(ahead, 0)

        @pl.when(i >= LAG + 2)
        def _():
            stage_finish(i - LAG - 2)

        @pl.when((i >= LAG + 1) & (i < units + LAG + 1))
        def _():
            stage_sum(i - LAG - 1)

        @pl.when((i >= LAG) & (i < units + LAG))
        def _():
            stage_pair(i - LAG)

        @pl.when(i < units)
        def _():
            stage_compute(i)

        return carry

    lax.fori_loop(0, units + LAG + 2, step, 0)

    def drain(unit, carry):
        side_copy(unit).wait_send()
        chip_copy(unit).wait_send()
        forward_up(unit, direct).wait_send()
        forward_down(unit, direct).wait_send()
        pair_copy(unit).wait_send()
        for way in range(2):
            relay_copy(way, unit).wait_send()
            sum_copy(way, unit).wait_send()
        return carry

    lax.fori_loop(0, units, drain, 0)


def body(wavefunction, left_env, right_env, block_dims, mpo_shift):
    vectors, slots, block, _ = wavefunction.shape
    slab, units = block // 8, 2 * slots
    left_env = left_env.reshape(2, slots, 4, 2, slab, block)
    bf16, f32 = jnp.bfloat16, jnp.float32
    smem = pl.BlockSpec(memory_space=pltpu.SMEM)
    anywhere = pl.BlockSpec(memory_space=pl.ANY)
    return pl.pallas_call(
        kernel,
        out_shape=jax.ShapeDtypeStruct((vectors, slots, slab, block), bf16),
        in_specs=[smem, smem, anywhere, anywhere, anywhere],
        out_specs=pl.BlockSpec(memory_space=pltpu.VMEM),
        scratch_shapes=[
            pltpu.VMEM((units, block, block), bf16),
            pltpu.VMEM((units, block, block), bf16),
            pltpu.VMEM((units, block, block), bf16),
            pltpu.VMEM((ENV_RING, 2, 4, 2, slab, block), bf16),
            pltpu.VMEM((ENV_RING, 2, block, block), bf16),
            pltpu.VMEM((2, block, block), bf16),
            pltpu.VMEM((2, block, block), bf16),
            pltpu.VMEM((units, 4, slab, block), bf16),
            pltpu.VMEM((units, 4, slab, block), bf16),
            pltpu.VMEM((RING, 4, slab, block), f32),
            pltpu.VMEM((2, units, slab // 2, block), bf16),
            pltpu.VMEM((2, units, slab // 2, block), bf16),
            pltpu.VMEM((2, units, slab, block), bf16),
            pltpu.VMEM((2, units, slab, block), bf16),
            pltpu.SemaphoreType.DMA((KINDS, units)),
            pltpu.SemaphoreType.DMA((KINDS, units)),
            pltpu.SemaphoreType.DMA((units,)),
            pltpu.SemaphoreType.DMA((ENV_RING,)),
            pltpu.SemaphoreType.DMA((ENV_RING,)),
        ],
        compiler_params=pltpu.CompilerParams(
            collective_id=0, has_side_effects=True, vmem_limit_bytes=66 * 1000 * 1000
        ),
        name="matvec",
    )(mpo_shift, block_dims, wavefunction, left_env, right_env)


def solution(mesh):
    placed = (
        P(None, "sec", None, None),
        P("mpo", "sec", None, None),
        P("mpo", "sec", None, None),
        P("sec"),
        P("mpo"),
    )
    return jax.shard_map(
        body, mesh=mesh, in_specs=placed, out_specs=P(None, "sec", "mpo", None), check_vma=False
    )
```

time: 159 us -> 132 us (0.83)
  the two profiles are of different devices: /device:TPU:30 before, /device:TPU:0 now
where the time goes in v2:
time: 132 us; the launch traced here: 130 us
  Pallas kernels  127 us (96%)
  local copies, waits for them, and re-layouts  2.29 us (2%)
    pallas_call x1, Pallas kernels, body(): pl.pallas_call(kernel, out_shape=jax.ShapeDtypeStruct((vectors, slots, sl...  127 us

profile of v2, /device:TPU:0, one launch (start us, length us, event | category | flops | bytes accessed | tf_op | source)
XLA Modules:
  0.0 129.7 jit_solution(5873642776168018322)
XLA Ops:
  0.0 127.4 %matvec.1 = bf16[2,8,64,512]{3,2,1,0:T(8,128)(2,1)} custom-call(s32[2]{0:T(128)} %shift_ref.1, s32[8]{0:T(128)} %dims_ref.1, bf16[2,8,512,512]{3,2,1,0:T(8,128)(2,1)} %wave_ref.1, bf16[2,8,4,2,64,512]{5,4,3,2,1,0:T(8,128)(2,1)} %bitcast.1, bf16[2,8,512,512]{3,2,1,0:T(8,128)(2,1)} %right_ref.1), custom_call_target="tpu_custom_call" | custom-call | tf_op jit(solution)/shard_map/matvec/pallas_call | solution.py:238
  127.4 2.3 %copy.7 = bf16[2,8,64,512]{3,2,1,0:T(8,128)(2,1)} copy(bf16[2,8,64,512]{3,2,1,0:T(8,128)(2,1)} %matvec.1) | data formatting | bytes 2097152

commit v3 on v2

v3 whole, which is shorter than its diff:
```python
import functools

import jax
import jax.numpy as jnp
from jax import lax
from jax.experimental import pallas as pl
from jax.experimental.pallas import tpu as pltpu
from jax.sharding import PartitionSpec as P

MESH = pl.DeviceIdType.MESH
LAG = 2
TAIL_LAG = 1
RING = LAG + 3
ENV_RING = 4
BY_QUARTER = 5
Z_FIRST = 2
Z_FROM, Z_STEP = 10, 5
CHIP, SIDE, FWD_UP, FWD_DOWN, HOP_UP, HOP_DOWN, RELAY_UP, RELAY_DOWN, SUM_UP, SUM_DOWN = range(10)
PAIR_FAR, PAIR_ABOVE, PAIR_BELOW, PAIR_OWN = range(10, 14)
KINDS = 14


def is_tail(unit):
    return (unit >= Z_FROM) & (unit % Z_STEP == Z_FROM % Z_STEP)


def tail_slot(unit):
    return (unit - Z_FROM) // Z_STEP


def kernel(
    shift_ref, dims_ref, wave_ref, left_ref, right_ref, out_ref,
    own, chip, side, left_buf, right_buf, chosen, parts,
    pair_send, pair_recv, total, relay_send, relay_recv, sum_send, sum_recv,
    tail_total, tail_relay_send, tail_relay_recv, tail_sum_send, tail_sum_recv, tail_pair_send, tail_pair_recv,
    send_sem, recv_sem, own_sem, left_sem, right_sem,
):
    bf16, f32 = jnp.bfloat16, jnp.float32
    slots, block = wave_ref.shape[1], wave_ref.shape[2]
    units = 2 * slots
    half, quarter, eighth = block // 2, block // 4, block // 8
    slab = block // 8
    mpo = lax.axis_index("mpo")
    sec = lax.axis_index("sec")
    secs = lax.axis_size("sec")
    core = sec % 2
    z = mpo // 2
    x_lo = mpo % 2
    above, below, far = (z + 1) % 4, (z + 3) % 4, (z + 2) % 4
    direct = (z % 2) * half
    indirect = half - direct
    up = ((mpo + 2) % 8, sec)
    down = ((mpo + 6) % 8, sec)
    pair = (mpo + 1 - 2 * x_lo, sec)
    chip_mate = (mpo, sec + 1 - 2 * core)
    side_mate = (mpo + 1 - 2 * x_lo, (sec + secs - 1 + 2 * core) % secs)
    first = (secs - 1 - sec) // (secs - 1)
    last = sec // (secs - 1)

    def remote(kind, unit, src, dst, device):
        return pltpu.make_async_remote_copy(
            src_ref=src, dst_ref=dst, send_sem=send_sem.at[kind, unit],
            recv_sem=recv_sem.at[kind, unit], device_id=device, device_id_type=MESH,
        )

    def chip_copy(unit):
        return remote(CHIP, unit, wave_ref.at[unit % 2, unit // 2], chip.at[unit], chip_mate)

    def side_copy(unit, start, size):
        source = (unit // 2 + first - last + slots) % slots
        rows = pl.ds(start, size)
        return remote(SIDE, unit, wave_ref.at[unit % 2, source, rows], side.at[unit, rows], side_mate)

    def pass_on(kind, unit, start, size, device):
        piece = side.at[unit, pl.ds(start, size)]
        return remote(kind, unit, piece, piece, device)

    def half_up(unit, start):
        return pass_on(FWD_UP, unit, start, quarter, up)

    def half_down(unit, start):
        return pass_on(FWD_DOWN, unit, start + quarter, quarter, down)

    def quarter_up(unit, layer):
        return pass_on(FWD_UP, unit, layer * quarter, quarter, up)

    def quarter_down(unit, layer):
        return pass_on(FWD_DOWN, unit, layer * quarter, quarter, down)

    def hop_up(unit, layer):
        return pass_on(HOP_UP, unit, layer * quarter, eighth, up)

    def hop_down(unit, layer):
        return pass_on(HOP_DOWN, unit, layer * quarter + eighth, eighth, down)

    def pair_copy(kind, unit):
        layer = {PAIR_FAR: far, PAIR_ABOVE: above, PAIR_BELOW: below, PAIR_OWN: z}[kind]
        return remote(kind, unit, pair_send.at[unit, layer], pair_recv.at[unit, layer], pair)

    def relay_copy(way, unit):
        return remote(RELAY_UP + way, unit, relay_send.at[way, unit], relay_recv.at[way, unit], (up, down)[way])

    def sum_copy(way, unit):
        return remote(SUM_UP + way, unit, sum_send.at[way, unit], sum_recv.at[way, unit], (up, down)[way])

    def tail_pair_copy(unit):
        at = tail_slot(unit)
        return remote(PAIR_OWN, unit, tail_pair_send.at[at], tail_pair_recv.at[at], pair)

    def tail_relay_copy(way, unit):
        at = tail_slot(unit)
        return remote(
            RELAY_UP + way, unit, tail_relay_send.at[way, at], tail_relay_recv.at[way, at], (up, down)[way]
        )

    def tail_sum_copy(way, unit):
        at = tail_slot(unit)
        return remote(SUM_UP + way, unit, tail_sum_send.at[way, at], tail_sum_recv.at[way, at], (up, down)[way])

    def own_copy(unit):
        return pltpu.make_async_copy(wave_ref.at[unit % 2, unit // 2], own.at[unit], own_sem.at[unit])

    def left_copy(slot):
        at = slot % ENV_RING
        return pltpu.make_async_copy(left_ref.at[:, slot], left_buf.at[at], left_sem.at[at])

    def right_copy(slot):
        at = slot % ENV_RING
        return pltpu.make_async_copy(right_ref.at[:, slot], right_buf.at[at], right_sem.at[at])

    barrier = pltpu.get_barrier_semaphore()
    for mate in (up, down, pair, chip_mate, side_mate):
        pl.semaphore_signal(barrier, inc=1, device_id=mate, device_id_type=MESH)

    def start_local(slot, carry):
        own_copy(2 * slot).start()
        own_copy(2 * slot + 1).start()
        left_copy(slot).start()
        right_copy(slot).start()
        return carry

    lax.fori_loop(0, ENV_RING - 1, start_local, 0)
    pl.semaphore_wait(barrier, 5)

    def start_quarters(unit, carry):
        side_copy(unit, z * quarter, quarter).start()
        chip_copy(unit).start()
        return carry

    def start_halves(unit, carry):
        side_copy(unit, direct, half).start()
        chip_copy(unit).start()
        return carry

    lax.fori_loop(0, BY_QUARTER, start_quarters, 0)
    lax.fori_loop(BY_QUARTER, units, start_halves, 0)

    def stage_quarter(unit):
        side_copy(unit, z * quarter, quarter).wait_recv()
        quarter_up(unit, z).start()
        quarter_down(unit, z).start()

    def stage_hop(unit):
        quarter_up(unit, below).wait_recv()
        hop_up(unit, below).start()
        quarter_down(unit, above).wait_recv()
        hop_down(unit, above).start()

    def stage_half(unit):
        side_copy(unit, direct, half).wait_recv()
        half_up(unit, direct).start()
        half_down(unit, direct).start()

    def write(unit, value):
        limit = dims_ref[unit // 2]
        rows = mpo * slab + lax.broadcasted_iota(jnp.int32, value.shape, 0)
        cols = lax.broadcasted_iota(jnp.int32, value.shape, 1)
        inside = (rows < limit) & (cols < limit)
        out_ref[unit % 2, unit // 2] = jnp.where(inside, value, jnp.zeros_like(value)).astype(bf16)

    top, bottom = pl.ds(0, slab // 2), pl.ds(slab // 2, slab // 2)

    def summed(unit, layer, rows=slice(None)):
        return total[unit % RING, layer, rows] + pair_recv[unit, layer, rows].astype(f32)

    def stage_finish(unit):
        pair_copy(PAIR_OWN, unit).wait_recv()
        sum_copy(0, unit).wait_recv()
        sum_copy(1, unit).wait_recv()
        value = summed(unit, z) + sum_recv[0, unit].astype(f32)
        write(unit, value + sum_recv[1, unit].astype(f32))

    def stage_sum(unit):
        pair_copy(PAIR_ABOVE, unit).wait_recv()
        relay_copy(0, unit).wait_recv()
        sum_send[0, unit, top] = (summed(unit, above, top) + relay_recv[0, unit].astype(f32)).astype(bf16)
        sum_send[0, unit, bottom] = summed(unit, above, bottom).astype(bf16)
        sum_copy(0, unit).start()
        pair_copy(PAIR_BELOW, unit).wait_recv()
        relay_copy(1, unit).wait_recv()
        sum_send[1, unit, top] = summed(unit, below, top).astype(bf16)
        sum_send[1, unit, bottom] = (summed(unit, below, bottom) + relay_recv[1, unit].astype(f32)).astype(bf16)
        sum_copy(1, unit).start()

    def stage_pair(unit):
        pair_copy(PAIR_FAR, unit).wait_recv()
        relay_send[0, unit] = summed(unit, far, top).astype(bf16)
        relay_copy(0, unit).start()
        relay_send[1, unit] = summed(unit, far, bottom).astype(bf16)
        relay_copy(1, unit).start()

    def tail_finish(unit):
        at = tail_slot(unit)
        tail_pair_copy(unit).wait_recv()
        write(unit, tail_total[at, 1, z] + tail_pair_recv[at].astype(f32))

    def tail_pair(unit):
        at = tail_slot(unit)
        tail_sum_copy(0, unit).wait_recv()
        tail_sum_copy(1, unit).wait_recv()
        for side_of in range(2):
            value = tail_total[at, side_of, z] + tail_sum_recv[0, at, side_of].astype(f32)
            value = value + tail_sum_recv[1, at, side_of].astype(f32)
            if side_of == 0:
                tail_pair_send[at] = value.astype(bf16)
                tail_pair_copy(unit).start()
            else:
                tail_total[at, 1, z] = value

    def tail_sum(unit):
        at = tail_slot(unit)
        tail_relay_copy(0, unit).wait_recv()
        tail_sum_send[0, at, 0] = (tail_total[at, 0, above] + tail_relay_recv[0, at].astype(f32)).astype(bf16)
        tail_sum_send[0, at, 1] = tail_total[at, 1, above].astype(bf16)
        tail_sum_copy(0, unit).start()
        tail_relay_copy(1, unit).wait_recv()
        tail_sum_send[1, at, 0] = tail_total[at, 0, below].astype(bf16)
        tail_sum_send[1, at, 1] = (tail_total[at, 1, below] + tail_relay_recv[1, at].astype(f32)).astype(bf16)
        tail_sum_copy(1, unit).start()

    def stage_compute(unit):
        slot = unit // 2
        at = slot % ENV_RING
        own_copy(unit).wait()

        @pl.when(unit % 2 == 0)
        def _():
            left_copy(slot).wait()
            right_copy(slot).wait()

        chip_copy(unit).wait_recv()

        @pl.when(unit < BY_QUARTER)
        def _():
            hop_up(unit, far).wait_recv()
            hop_down(unit, far).wait_recv()

        @pl.when(unit >= BY_QUARTER)
        def _():
            half_up(unit, indirect).wait_recv()
            half_down(unit, indirect).wait_recv()

        missing = first * ((slots - 1 - slot) // (slots - 1)) + last * (slot // (slots - 1))
        for w in range(2):
            turn = shift_ref[w] * (1 - 2 * core)
            use_side = (turn == 1).astype(f32) * (1 - missing).astype(f32)
            use_chip = (turn == -1).astype(f32)
            use_own = (turn == 0).astype(f32)
            chosen[w] = (
                own[unit] * use_own.astype(bf16)
                + chip[unit] * use_chip.astype(bf16)
                + side[unit] * use_side.astype(bf16)
            )
            theirs = left_buf[at, w, :, 1 - x_lo].reshape(half, block)
            mine = left_buf[at, w, :, x_lo].reshape(half, block)
            rows = jnp.concatenate([theirs, mine], axis=0)
            parts[w] = jnp.dot(rows, chosen[w], preferred_element_type=f32).astype(bf16)
        both = jnp.dot(parts[0], right_buf[at, 0], preferred_element_type=f32) + jnp.dot(
            parts[1], right_buf[at, 1], preferred_element_type=f32
        )

        @pl.when(jnp.logical_not(is_tail(unit)))
        def _():
            pair_send[unit] = both[:half].astype(bf16).reshape(4, slab, block)
            for kind in (PAIR_FAR, PAIR_ABOVE, PAIR_BELOW, PAIR_OWN):
                pair_copy(kind, unit).start()
            total[unit % RING] = both[half:].reshape(4, slab, block)

        @pl.when(is_tail(unit))
        def _():
            tail = tail_slot(unit)
            tail_total[tail] = both.reshape(2, 4, slab, block)
            for way in range(2):
                tail_relay_send[way, tail] = tail_total[tail, way, far].astype(bf16)
                tail_relay_copy(way, unit).start()

    def step(i, carry):
        @pl.when(i < BY_QUARTER)
        def _():
            stage_quarter(i)

        @pl.when((i >= BY_QUARTER) & (i < units))
        def _():
            stage_half(i)

        now = i - 2
        ahead = now // 2 + ENV_RING - 1

        @pl.when((now >= 0) & (now % 2 == 0) & (ahead < slots))
        def _():
            start_local(ahead, 0)

        def later(lag, tail, stage):
            unit = now - lag
            kind = is_tail(unit) if tail else jnp.logical_not(is_tail(unit))

            @pl.when((unit >= 0) & (unit < units) & kind)
            def _():
                stage(unit)

        later(LAG + 2, False, stage_finish)
        later(LAG + 1, False, stage_sum)
        later(TAIL_LAG + 2, True, tail_finish)
        later(LAG, False, stage_pair)
        later(TAIL_LAG + 1, True, tail_pair)
        later(TAIL_LAG, True, tail_sum)

        @pl.when((i >= 1) & (i < BY_QUARTER + 1))
        def _():
            stage_hop(i - 1)

        @pl.when((now >= 0) & (now < units))
        def _():
            stage_compute(now)

        return carry

    lax.fori_loop(0, 2 + units + LAG + 2, step, 0)

    def drain_quarters(unit, carry):
        side_copy(unit, z * quarter, quarter).wait_send()
        quarter_up(unit, z).wait_send()
        quarter_down(unit, z).wait_send()
        hop_up(unit, below).wait_send()
        hop_down(unit, above).wait_send()
        return carry

    def drain_halves(unit, carry):
        side_copy(unit, direct, half).wait_send()
        half_up(unit, direct).wait_send()
        half_down(unit, direct).wait_send()
        return carry

    def drain_sums(unit, carry):
        chip_copy(unit).wait_send()

        @pl.when(jnp.logical_not(is_tail(unit)))
        def _():
            for kind in (PAIR_FAR, PAIR_ABOVE, PAIR_BELOW, PAIR_OWN):
                pair_copy(kind, unit).wait_send()
            for way in range(2):
                relay_copy(way, unit).wait_send()
                sum_copy(way, unit).wait_send()

        @pl.when(is_tail(unit))
        def _():
            tail_pair_copy(unit).wait_send()
            for way in range(2):
                tail_relay_copy(way, unit).wait_send()
                tail_sum_copy(way, unit).wait_send()

        return carry

    lax.fori_loop(0, BY_QUARTER, drain_quarters, 0)
    lax.fori_loop(BY_QUARTER, units, drain_halves, 0)
    lax.fori_loop(0, units, drain_sums, 0)


def body(wavefunction, left_env, right_env, block_dims, mpo_shift):
    vectors, slots, block, _ = wavefunction.shape
    slab, units = block // 8, 2 * slots
    left_env = left_env.reshape(2, slots, 4, 2, slab, block)
    bf16, f32 = jnp.bfloat16, jnp.float32
    smem = pl.BlockSpec(memory_space=pltpu.SMEM)
    anywhere = pl.BlockSpec(memory_space=pl.ANY)
    return pl.pallas_call(
        kernel,
        out_shape=jax.ShapeDtypeStruct((vectors, slots, slab, block), bf16),
        in_specs=[smem, smem, anywhere, anywhere, anywhere],
        out_specs=pl.BlockSpec(memory_space=pltpu.VMEM),
        scratch_shapes=[
            pltpu.VMEM((units, block, block), bf16),
            pltpu.VMEM((units, block, block), bf16),
            pltpu.VMEM((units, block, block), bf16),
            pltpu.VMEM((ENV_RING, 2, 4, 2, slab, block), bf16),
            pltpu.VMEM((ENV_RING, 2, block, block), bf16),
            pltpu.VMEM((2, block, block), bf16),
            pltpu.VMEM((2, block, block), bf16),
            pltpu.VMEM((units, 4, slab, block), bf16),
            pltpu.VMEM((units, 4, slab, block), bf16),
            pltpu.VMEM((RING, 4, slab, block), f32),
            pltpu.VMEM((2, units, slab // 2, block), bf16),
            pltpu.VMEM((2, units, slab // 2, block), bf16),
            pltpu.VMEM((2, units, slab, block), bf16),
            pltpu.VMEM((2, units, slab, block), bf16),
            pltpu.VMEM((Z_FIRST, 2, 4, slab, block), f32),
            pltpu.VMEM((2, Z_FIRST, slab, block), bf16),
            pltpu.VMEM((2, Z_FIRST, slab, block), bf16),
            pltpu.VMEM((2, Z_FIRST, 2, slab, block), bf16),
            pltpu.VMEM((2, Z_FIRST, 2, slab, block), bf16),
            pltpu.VMEM((Z_FIRST, slab, block), bf16),
            pltpu.VMEM((Z_FIRST, slab, block), bf16),
            pltpu.SemaphoreType.DMA((KINDS, units)),
            pltpu.SemaphoreType.DMA((KINDS, units)),
            pltpu.SemaphoreType.DMA((units,)),
            pltpu.SemaphoreType.DMA((ENV_RING,)),
            pltpu.SemaphoreType.DMA((ENV_RING,)),
        ],
        compiler_params=pltpu.CompilerParams(
            collective_id=0, has_side_effects=True, vmem_limit_bytes=66 * 1000 * 1000
        ),
        name="matvec",
    )(mpo_shift, block_dims, wavefunction, left_env, right_env)


def solution(mesh):
    placed = (
        P(None, "sec", None, None),
        P("mpo", "sec", None, None),
        P("mpo", "sec", None, None),
        P("sec"),
        P("mpo"),
    )
    return jax.shard_map(
        body, mesh=mesh, in_specs=placed, out_specs=P(None, "sec", "mpo", None), check_vma=False
    )
```

time: 132 us -> 120 us (0.909); the launches traced: 130 us -> 120 us
  Pallas kernels: 127 us -> 117 us
    pallas_call x1, Pallas kernels: 127 us -> 117 us  [body(): pl.pallas_call(kernel, out_shape=jax.ShapeDtypeStruct((vectors, slots, sl...]
where the time goes in v3:
time: 120 us
  Pallas kernels  117 us (98%)
  local copies, waits for them, and re-layouts  2.29 us (2%)
    pallas_call x1, Pallas kernels, body(): pl.pallas_call(kernel, out_shape=jax.ShapeDtypeStruct((vectors, slots, sl...  117 us

profile of v3, /device:TPU:0, one launch (start us, length us, event | category | flops | bytes accessed | tf_op | source)
XLA Modules:
  0.0 119.7 jit_solution(692591710539197685)
XLA Ops:
  0.0 117.4 %matvec.1 = bf16[2,8,64,512]{3,2,1,0:T(8,128)(2,1)} custom-call(s32[2]{0:T(128)} %shift_ref.1, s32[8]{0:T(128)} %dims_ref.1, bf16[2,8,512,512]{3,2,1,0:T(8,128)(2,1)} %wave_ref.1, bf16[2,8,4,2,64,512]{5,4,3,2,1,0:T(8,128)(2,1)} %bitcast.1, bf16[2,8,512,512]{3,2,1,0:T(8,128)(2,1)} %right_ref.1), custom_call_target="tpu_custom_call" | custom-call | tf_op jit(solution)/shard_map/matvec/pallas_call | solution.py:386
  117.5 2.3 %copy.7 = bf16[2,8,64,512]{3,2,1,0:T(8,128)(2,1)} copy(bf16[2,8,64,512]{3,2,1,0:T(8,128)(2,1)} %matvec.1) | data formatting | bytes 2097152

commit v4 on v3

--- a/solution.py
+++ b/solution.py
@@ -8,24 +8,33 @@
 from jax.sharding import PartitionSpec as P
 
 MESH = pl.DeviceIdType.MESH
-LAG = 2
-TAIL_LAG = 1
-RING = LAG + 3
+LAGS = (2, 4, 5)
+TAIL_LAGS = (1, 3, 4)
+AHEAD = 2
+RING = max(LAGS) + 1
 ENV_RING = 4
-BY_QUARTER = 5
-Z_FIRST = 2
-Z_FROM, Z_STEP = 10, 5
+BY_QUARTER = (0, 1, 2, 3, 4, 10, 12)
+WHOLE = (11, 15)
+Z_FIRST = (8, 13, 15)
+Z_SLOTS = next(n for n in range(len(Z_FIRST), 17) if len({u % n for u in Z_FIRST}) == len(Z_FIRST))
 CHIP, SIDE, FWD_UP, FWD_DOWN, HOP_UP, HOP_DOWN, RELAY_UP, RELAY_DOWN, SUM_UP, SUM_DOWN = range(10)
 PAIR_FAR, PAIR_ABOVE, PAIR_BELOW, PAIR_OWN = range(10, 14)
 KINDS = 14
 
 
+def one_of(unit, members):
+    found = unit == members[0]
+    for member in members[1:]:
+        found = found | (unit == member)
+    return found
+
+
 def is_tail(unit):
-    return (unit >= Z_FROM) & (unit % Z_STEP == Z_FROM % Z_STEP)
+    return one_of(unit, Z_FIRST)
 
 
 def tail_slot(unit):
-    return (unit - Z_FROM) // Z_STEP
+    return unit % Z_SLOTS
 
 
 def kernel(
@@ -33,7 +42,7 @@
     own, chip, side, left_buf, right_buf, chosen, parts,
     pair_send, pair_recv, total, relay_send, relay_recv, sum_send, sum_recv,
     tail_total, tail_relay_send, tail_relay_recv, tail_sum_send, tail_sum_recv, tail_pair_send, tail_pair_recv,
-    send_sem, recv_sem, own_sem, left_sem, right_sem,
+    out_buf, send_sem, recv_sem, own_sem, left_sem, right_sem, out_sem,
 ):
     bf16, f32 = jnp.bfloat16, jnp.float32
     slots, block = wave_ref.shape[1], wave_ref.shape[2]
@@ -120,6 +129,9 @@
     def own_copy(unit):
         return pltpu.make_async_copy(wave_ref.at[unit % 2, unit // 2], own.at[unit], own_sem.at[unit])
 
+    def out_copy(unit):
+        return pltpu.make_async_copy(out_buf.at[unit], out_ref.at[unit % 2, unit // 2], out_sem.at[unit])
+
     def left_copy(slot):
         at = slot % ENV_RING
         return pltpu.make_async_copy(left_ref.at[:, slot], left_buf.at[at], left_sem.at[at])
@@ -142,18 +154,26 @@
     lax.fori_loop(0, ENV_RING - 1, start_local, 0)
     pl.semaphore_wait(barrier, 5)
 
-    def start_quarters(unit, carry):
-        side_copy(unit, z * quarter, quarter).start()
+    def by_kind(unit, quarters, whole, halves):
+        is_quarter, is_whole = one_of(unit, BY_QUARTER), one_of(unit, WHOLE)
+        inside = (unit >= 0) & (unit < units)
+        pl.when(is_quarter)(quarters)
+        if whole is not None:
+            pl.when(is_whole)(whole)
+        if halves is not None:
+            pl.when(inside & jnp.logical_not(is_quarter | is_whole))(halves)
+
+    def start_remote(unit, carry):
+        by_kind(
+            unit,
+            lambda: side_copy(unit, z * quarter, quarter).start(),
+            lambda: side_copy(unit, 0, block).start(),
+            lambda: side_copy(unit, direct, half).start(),
+        )
         chip_copy(unit).start()
         return carry
 
-    def start_halves(unit, carry):
-        side_copy(unit, direct, half).start()
-        chip_copy(unit).start()
-        return carry
-
-    lax.fori_loop(0, BY_QUARTER, start_quarters, 0)
-    lax.fori_loop(BY_QUARTER, units, start_halves, 0)
+    lax.fori_loop(0, units, start_remote, 0)
 
     def stage_quarter(unit):
         side_copy(unit, z * quarter, quarter).wait_recv()
@@ -176,7 +196,8 @@
         rows = mpo * slab + lax.broadcasted_iota(jnp.int32, value.shape, 0)
         cols = lax.broadcasted_iota(jnp.int32, value.shape, 1)
         inside = (rows < limit) & (cols < limit)
-        out_ref[unit % 2, unit // 2] = jnp.where(inside, value, jnp.zeros_like(value)).astype(bf16)
+        out_buf[unit] = jnp.where(inside, value, jnp.zeros_like(value)).astype(bf16)
+        out_copy(unit).start()
 
     top, bottom = pl.ds(0, slab // 2), pl.ds(slab // 2, slab // 2)
 
@@ -250,15 +271,15 @@
 
         chip_copy(unit).wait_recv()
 
-        @pl.when(unit < BY_QUARTER)
-        def _():
+        def wait_hops():
             hop_up(unit, far).wait_recv()
             hop_down(unit, far).wait_recv()
 
-        @pl.when(unit >= BY_QUARTER)
-        def _():
+        def wait_halves():
             half_up(unit, indirect).wait_recv()
             half_down(unit, indirect).wait_recv()
+
+        by_kind(unit, wait_hops, lambda: side_copy(unit, 0, block).wait_recv(), wait_halves)
 
         missing = first * ((slots - 1 - slot) // (slots - 1)) + last * (slot // (slots - 1))
         for w in range(2):
@@ -295,15 +316,8 @@
                 tail_relay_copy(way, unit).start()
 
     def step(i, carry):
-        @pl.when(i < BY_QUARTER)
-        def _():
-            stage_quarter(i)
-
-        @pl.when((i >= BY_QUARTER) & (i < units))
-        def _():
-            stage_half(i)
-
-        now = i - 2
+        now = i - AHEAD
+        by_kind(i, lambda: stage_quarter(i), None, lambda: stage_half(i))
         ahead = now // 2 + ENV_RING - 1
 
         @pl.when((now >= 0) & (now % 2 == 0) & (ahead < slots))
@@ -318,16 +332,12 @@
             def _():
                 stage(unit)
 
-        later(LAG + 2, False, stage_finish)
-        later(LAG + 1, False, stage_sum)
-        later(TAIL_LAG + 2, True, tail_finish)
-        later(LAG, False, stage_pair)
-        later(TAIL_LAG + 1, True, tail_pair)
-        later(TAIL_LAG, True, tail_sum)
-
-        @pl.when((i >= 1) & (i < BY_QUARTER + 1))
-        def _():
-            stage_hop(i - 1)
+        stages = list(zip(LAGS, (False,) * 3, (stage_pair, stage_sum, stage_finish)))
+        stages += zip(TAIL_LAGS, (True,) * 3, (tail_sum, tail_pair, tail_finish))
+        for lag, tail, stage in sorted(stages, key=lambda item: -item[0]):
+            later(lag, tail, stage)
+
+        by_kind(now + 1, lambda: stage_hop(now + 1), None, None)
 
         @pl.when((now >= 0) & (now < units))
         def _():
@@ -335,23 +345,28 @@
 
         return carry
 
-    lax.fori_loop(0, 2 + units + LAG + 2, step, 0)
-
-    def drain_quarters(unit, carry):
+    lax.fori_loop(0, AHEAD + units + max(max(LAGS), max(TAIL_LAGS)), step, 0)
+
+    def drain_quarters(unit):
         side_copy(unit, z * quarter, quarter).wait_send()
         quarter_up(unit, z).wait_send()
         quarter_down(unit, z).wait_send()
         hop_up(unit, below).wait_send()
         hop_down(unit, above).wait_send()
-        return carry
-
-    def drain_halves(unit, carry):
+
+    def drain_halves(unit):
         side_copy(unit, direct, half).wait_send()
         half_up(unit, direct).wait_send()
         half_down(unit, direct).wait_send()
-        return carry
-
-    def drain_sums(unit, carry):
+
+    def drain(unit, carry):
+        by_kind(
+            unit,
+            lambda: drain_quarters(unit),
+            lambda: side_copy(unit, 0, block).wait_send(),
+            lambda: drain_halves(unit),
+        )
+        out_copy(unit).wait()
         chip_copy(unit).wait_send()
 
         @pl.when(jnp.logical_not(is_tail(unit)))
@@ -371,9 +386,7 @@
 
         return carry
 
-    lax.fori_loop(0, BY_QUARTER, drain_quarters, 0)
-    lax.fori_loop(BY_QUARTER, units, drain_halves, 0)
-    lax.fori_loop(0, units, drain_sums, 0)
+    lax.fori_loop(0, units, drain, 0)
 
 
 def body(wavefunction, left_env, right_env, block_dims, mpo_shift):
@@ -387,7 +400,7 @@
         kernel,
         out_shape=jax.ShapeDtypeStruct((vectors, slots, slab, block), bf16),
         in_specs=[smem, smem, anywhere, anywhere, anywhere],
-        out_specs=pl.BlockSpec(memory_space=pltpu.VMEM),
+        out_specs=anywhere,
         scratch_shapes=[
             pltpu.VMEM((units, block, block), bf16),
             pltpu.VMEM((units, block, block), bf16),
@@ -403,18 +416,20 @@
             pltpu.VMEM((2, units, slab // 2, block), bf16),
             pltpu.VMEM((2, units, slab, block), bf16),
             pltpu.VMEM((2, units, slab, block), bf16),
-            pltpu.VMEM((Z_FIRST, 2, 4, slab, block), f32),
-            pltpu.VMEM((2, Z_FIRST, slab, block), bf16),
-            pltpu.VMEM((2, Z_FIRST, slab, block), bf16),
-            pltpu.VMEM((2, Z_FIRST, 2, slab, block), bf16),
-            pltpu.VMEM((2, Z_FIRST, 2, slab, block), bf16),
-            pltpu.VMEM((Z_FIRST, slab, block), bf16),
-            pltpu.VMEM((Z_FIRST, slab, block), bf16),
+            pltpu.VMEM((Z_SLOTS, 2, 4, slab, block), f32),
+            pltpu.VMEM((2, Z_SLOTS, slab, block), bf16),
+            pltpu.VMEM((2, Z_SLOTS, slab, block), bf16),
+            pltpu.VMEM((2, Z_SLOTS, 2, slab, block), bf16),
+            pltpu.VMEM((2, Z_SLOTS, 2, slab, block), bf16),
+            pltpu.VMEM((Z_SLOTS, slab, block), bf16),
+            pltpu.VMEM((Z_SLOTS, slab, block), bf16),
+            pltpu.VMEM((units, slab, block), bf16),
             pltpu.SemaphoreType.DMA((KINDS, units)),
             pltpu.SemaphoreType.DMA((KINDS, units)),
             pltpu.SemaphoreType.DMA((units,)),
             pltpu.SemaphoreType.DMA((ENV_RING,)),
             pltpu.SemaphoreType.DMA((ENV_RING,)),
+            pltpu.SemaphoreType.DMA((units,)),
         ],
         compiler_params=pltpu.CompilerParams(
             collective_id=0, has_side_effects=True, vmem_limit_bytes=66 * 1000 * 1000

time: 120 us -> 116 us (0.967)
  Pallas kernels: 117 us -> 114 us
    pallas_call x1, Pallas kernels: 117 us -> 114 us  [body(): pl.pallas_call(kernel, out_shape=jax.ShapeDtypeStruct((vectors, slots, sl...]
where the time goes in v4:
time: 116 us
  Pallas kernels  114 us (98%)
  local copies, waits for them, and re-layouts  2.29 us (2%)
    pallas_call x1, Pallas kernels, body(): pl.pallas_call(kernel, out_shape=jax.ShapeDtypeStruct((vectors, slots, sl...  114 us

profile of v4, /device:TPU:0, one launch (start us, length us, event | category | flops | bytes accessed | tf_op | source)
XLA Modules:
  0.0 116.2 jit_solution(9091492692218728131)
XLA Ops:
  0.0 113.9 %matvec.1 = bf16[2,8,64,512]{3,2,1,0:T(8,128)(2,1)} custom-call(s32[2]{0:T(128)} %shift_ref.1, s32[8]{0:T(128)} %dims_ref.1, bf16[2,8,512,512]{3,2,1,0:T(8,128)(2,1)} %wave_ref.1, bf16[2,8,4,2,64,512]{5,4,3,2,1,0:T(8,128)(2,1)} %bitcast.1, bf16[2,8,512,512]{3,2,1,0:T(8,128)(2,1)} %right_ref.1), custom_call_target="tpu_custom_call" | custom-call | tf_op jit(solution)/shard_map/matvec/pallas_call | solution.py:399
  114.0 2.3 %copy.7 = bf16[2,8,64,512]{3,2,1,0:T(8,128)(2,1)} copy(bf16[2,8,64,512]{3,2,1,0:T(8,128)(2,1)} %matvec.1) | data formatting | bytes 2097152

commit v5 on v4

--- a/solution.py
+++ b/solution.py
@@ -8,15 +8,16 @@
 from jax.sharding import PartitionSpec as P
 
 MESH = pl.DeviceIdType.MESH
-LAGS = (2, 4, 5)
-TAIL_LAGS = (1, 3, 4)
+LAGS = (2, 3, 5)
+TAIL_LAGS = (2, 4, 6)
 AHEAD = 2
+DRAIN_LAG = max(LAGS + TAIL_LAGS) + 1
 RING = max(LAGS) + 1
 ENV_RING = 4
-BY_QUARTER = (0, 1, 2, 3, 4, 10, 12)
-WHOLE = (11, 15)
-Z_FIRST = (8, 13, 15)
-Z_SLOTS = next(n for n in range(len(Z_FIRST), 17) if len({u % n for u in Z_FIRST}) == len(Z_FIRST))
+BY_QUARTER = (0, 1, 2, 3, 5, 6, 11, 12)
+WHOLE = (13, 14, 15)
+Z_FIRST = (10, 13, 14)
+Z_SLOTS = len(Z_FIRST)
 CHIP, SIDE, FWD_UP, FWD_DOWN, HOP_UP, HOP_DOWN, RELAY_UP, RELAY_DOWN, SUM_UP, SUM_DOWN = range(10)
 PAIR_FAR, PAIR_ABOVE, PAIR_BELOW, PAIR_OWN = range(10, 14)
 KINDS = 14
@@ -34,7 +35,7 @@
 
 
 def tail_slot(unit):
-    return unit % Z_SLOTS
+    return sum((unit > member).astype(jnp.int32) for member in Z_FIRST[:-1])
 
 
 def kernel(
@@ -315,38 +316,6 @@
                 tail_relay_send[way, tail] = tail_total[tail, way, far].astype(bf16)
                 tail_relay_copy(way, unit).start()
 
-    def step(i, carry):
-        now = i - AHEAD
-        by_kind(i, lambda: stage_quarter(i), None, lambda: stage_half(i))
-        ahead = now // 2 + ENV_RING - 1
-
-        @pl.when((now >= 0) & (now % 2 == 0) & (ahead < slots))
-        def _():
-            start_local(ahead, 0)
-
-        def later(lag, tail, stage):
-            unit = now - lag
-            kind = is_tail(unit) if tail else jnp.logical_not(is_tail(unit))
-
-            @pl.when((unit >= 0) & (unit < units) & kind)
-            def _():
-                stage(unit)
-
-        stages = list(zip(LAGS, (False,) * 3, (stage_pair, stage_sum, stage_finish)))
-        stages += zip(TAIL_LAGS, (True,) * 3, (tail_sum, tail_pair, tail_finish))
-        for lag, tail, stage in sorted(stages, key=lambda item: -item[0]):
-            later(lag, tail, stage)
-
-        by_kind(now + 1, lambda: stage_hop(now + 1), None, None)
-
-        @pl.when((now >= 0) & (now < units))
-        def _():
-            stage_compute(now)
-
-        return carry
-
-    lax.fori_loop(0, AHEAD + units + max(max(LAGS), max(TAIL_LAGS)), step, 0)
-
     def drain_quarters(unit):
         side_copy(unit, z * quarter, quarter).wait_send()
         quarter_up(unit, z).wait_send()
@@ -359,7 +328,7 @@
         half_up(unit, direct).wait_send()
         half_down(unit, direct).wait_send()
 
-    def drain(unit, carry):
+    def drain(unit):
         by_kind(
             unit,
             lambda: drain_quarters(unit),
@@ -384,9 +353,43 @@
                 tail_relay_copy(way, unit).wait_send()
                 tail_sum_copy(way, unit).wait_send()
 
+    def step(i, carry):
+        now = i - AHEAD
+        by_kind(i, lambda: stage_quarter(i), None, lambda: stage_half(i))
+        ahead = now // 2 + ENV_RING - 1
+
+        @pl.when((now >= 0) & (now % 2 == 0) & (ahead < slots))
+        def _():
+            start_local(ahead, 0)
+
+        def later(lag, tail, stage):
+            unit = now - lag
+            kind = is_tail(unit) if tail else jnp.logical_not(is_tail(unit))
+
+            @pl.when((unit >= 0) & (unit < units) & kind)
+            def _():
+                stage(unit)
+
+        stages = list(zip(LAGS, (False,) * 3, (stage_pair, stage_sum, stage_finish)))
+        stages += zip(TAIL_LAGS, (True,) * 3, (tail_sum, tail_pair, tail_finish))
+        for lag, tail, stage in sorted(stages, key=lambda item: -item[0]):
+            later(lag, tail, stage)
+
+        by_kind(now + 1, lambda: stage_hop(now + 1), None, None)
+
+        @pl.when((now >= 0) & (now < units))
+        def _():
+            stage_compute(now)
+
+        done = now - DRAIN_LAG
+
+        @pl.when((done >= 0) & (done < units))
+        def _():
+            drain(done)
+
         return carry
 
-    lax.fori_loop(0, units, drain, 0)
+    lax.fori_loop(0, AHEAD + units + DRAIN_LAG, step, 0)
 
 
 def body(wavefunction, left_env, right_env, block_dims, mpo_shift):

time: 116 us -> 115 us (level)
  Pallas kernels: 114 us -> 112 us
    pallas_call x1, Pallas kernels: 114 us -> 112 us  [body(): pl.pallas_call(kernel, out_shape=jax.ShapeDtypeStruct((vectors, slots, sl...]
where the time goes in v5:
time: 115 us; the launch traced here: 114 us
  Pallas kernels  112 us (97%)
  local copies, waits for them, and re-layouts  2.29 us (2%)
    pallas_call x1, Pallas kernels, body(): pl.pallas_call(kernel, out_shape=jax.ShapeDtypeStruct((vectors, slots, sl...  112 us

profile of v5, /device:TPU:0, one launch (start us, length us, event | category | flops | bytes accessed | tf_op | source)
XLA Modules:
  0.0 114.5 jit_solution(6669015726860312838)
XLA Ops:
  0.0 112.2 %matvec.1 = bf16[2,8,64,512]{3,2,1,0:T(8,128)(2,1)} custom-call(s32[2]{0:T(128)} %shift_ref.1, s32[8]{0:T(128)} %dims_ref.1, bf16[2,8,512,512]{3,2,1,0:T(8,128)(2,1)} %wave_ref.1, bf16[2,8,4,2,64,512]{5,4,3,2,1,0:T(8,128)(2,1)} %bitcast.1, bf16[2,8,512,512]{3,2,1,0:T(8,128)(2,1)} %right_ref.1), custom_call_target="tpu_custom_call" | custom-call | tf_op jit(solution)/shard_map/matvec/pallas_call | solution.py:402
  112.2 2.3 %copy.7 = bf16[2,8,64,512]{3,2,1,0:T(8,128)(2,1)} copy(bf16[2,8,64,512]{3,2,1,0:T(8,128)(2,1)} %matvec.1) | data formatting | bytes 2097152

commit v6 on v5

--- a/solution.py
+++ b/solution.py
@@ -8,19 +8,20 @@
 from jax.sharding import PartitionSpec as P
 
 MESH = pl.DeviceIdType.MESH
-LAGS = (2, 3, 5)
+LAGS = (2, 4, 6)
 TAIL_LAGS = (2, 4, 6)
 AHEAD = 2
 DRAIN_LAG = max(LAGS + TAIL_LAGS) + 1
 RING = max(LAGS) + 1
-ENV_RING = 4
-BY_QUARTER = (0, 1, 2, 3, 5, 6, 11, 12)
-WHOLE = (13, 14, 15)
-Z_FIRST = (10, 13, 14)
+ENV_RING = 3
+BY_QUARTER = (3, 4, 10, 13)
+THROUGH_PAIR = (0, 1, 2, 5, 6)
+WHOLE = (12, 14, 15)
+Z_FIRST = (2, 8, 11, 14)
 Z_SLOTS = len(Z_FIRST)
 CHIP, SIDE, FWD_UP, FWD_DOWN, HOP_UP, HOP_DOWN, RELAY_UP, RELAY_DOWN, SUM_UP, SUM_DOWN = range(10)
-PAIR_FAR, PAIR_ABOVE, PAIR_BELOW, PAIR_OWN = range(10, 14)
-KINDS = 14
+PAIR_FAR, PAIR_ABOVE, PAIR_BELOW, PAIR_OWN, FWD_PAIR = range(10, 15)
+KINDS = 15
 
 
 def one_of(unit, members):
@@ -59,6 +60,8 @@
     above, below, far = (z + 1) % 4, (z + 3) % 4, (z + 2) % 4
     direct = (z % 2) * half
     indirect = half - direct
+    near_mine, near_theirs = direct + x_lo * quarter, direct + (1 - x_lo) * quarter
+    off_mine, off_theirs = indirect + x_lo * quarter, indirect + (1 - x_lo) * quarter
     up = ((mpo + 2) % 8, sec)
     down = ((mpo + 6) % 8, sec)
     pair = (mpo + 1 - 2 * x_lo, sec)
@@ -155,19 +158,18 @@
     lax.fori_loop(0, ENV_RING - 1, start_local, 0)
     pl.semaphore_wait(barrier, 5)
 
-    def by_kind(unit, quarters, whole, halves):
-        is_quarter, is_whole = one_of(unit, BY_QUARTER), one_of(unit, WHOLE)
-        inside = (unit >= 0) & (unit < units)
-        pl.when(is_quarter)(quarters)
-        if whole is not None:
-            pl.when(is_whole)(whole)
-        if halves is not None:
-            pl.when(inside & jnp.logical_not(is_quarter | is_whole))(halves)
+    def by_kind(unit, quarters=None, through=None, whole=None, halves=None):
+        kinds = [one_of(unit, members) for members in (BY_QUARTER, THROUGH_PAIR, WHOLE)]
+        kinds.append((unit >= 0) & (unit < units) & jnp.logical_not(kinds[0] | kinds[1] | kinds[2]))
+        for found, action in zip(kinds, (quarters, through, whole, halves)):
+            if action is not None:
+                pl.when(found)(action)
 
     def start_remote(unit, carry):
         by_kind(
             unit,
             lambda: side_copy(unit, z * quarter, quarter).start(),
+            lambda: side_copy(unit, near_theirs, quarter).start(),
             lambda: side_copy(unit, 0, block).start(),
             lambda: side_copy(unit, direct, half).start(),
         )
@@ -186,6 +188,31 @@
         hop_up(unit, below).start()
         quarter_down(unit, above).wait_recv()
         hop_down(unit, above).start()
+
+    def through_pair(unit, near):
+        return [pass_on(FWD_PAIR, unit, near, quarter, pair)]
+
+    def through_forward(unit, near):
+        return [
+            pass_on(FWD_UP, unit, near, eighth, up),
+            pass_on(FWD_DOWN, unit, near + eighth, eighth, down),
+        ]
+
+    def through_hop(unit, off):
+        return [
+            pass_on(HOP_UP, unit, off, eighth, up),
+            pass_on(HOP_DOWN, unit, off + eighth, eighth, down),
+        ]
+
+    def stage_through(unit):
+        side_copy(unit, near_mine, quarter).wait_recv()
+        for copy in through_pair(unit, near_mine) + through_forward(unit, near_mine):
+            copy.start()
+
+    def stage_through_hop(unit):
+        through_pair(unit, near_theirs)[0].wait_recv()
+        for copy in through_hop(unit, near_theirs):
+            copy.start()
 
     def stage_half(unit):
         side_copy(unit, direct, half).wait_recv()
@@ -280,7 +307,11 @@
             half_up(unit, indirect).wait_recv()
             half_down(unit, indirect).wait_recv()
 
-        by_kind(unit, wait_hops, lambda: side_copy(unit, 0, block).wait_recv(), wait_halves)
+        def wait_through():
+            for copy in through_forward(unit, off_mine) + through_hop(unit, off_theirs):
+                copy.wait_recv()
+
+        by_kind(unit, wait_hops, wait_through, lambda: side_copy(unit, 0, block).wait_recv(), wait_halves)
 
         missing = first * ((slots - 1 - slot) // (slots - 1)) + last * (slot // (slots - 1))
         for w in range(2):
@@ -323,6 +354,12 @@
         hop_up(unit, below).wait_send()
         hop_down(unit, above).wait_send()
 
+    def drain_through(unit):
+        side_copy(unit, near_theirs, quarter).wait_send()
+        copies = through_pair(unit, near_mine) + through_forward(unit, near_mine)
+        for copy in copies + through_hop(unit, near_theirs):
+            copy.wait_send()
+
     def drain_halves(unit):
         side_copy(unit, direct, half).wait_send()
         half_up(unit, direct).wait_send()
@@ -332,6 +369,7 @@
         by_kind(
             unit,
             lambda: drain_quarters(unit),
+            lambda: drain_through(unit),
             lambda: side_copy(unit, 0, block).wait_send(),
             lambda: drain_halves(unit),
         )
@@ -355,7 +393,7 @@
 
     def step(i, carry):
         now = i - AHEAD
-        by_kind(i, lambda: stage_quarter(i), None, lambda: stage_half(i))
+        by_kind(i, lambda: stage_quarter(i), lambda: stage_through(i), None, lambda: stage_half(i))
         ahead = now // 2 + ENV_RING - 1
 
         @pl.when((now >= 0) & (now % 2 == 0) & (ahead < slots))
@@ -375,7 +413,7 @@
         for lag, tail, stage in sorted(stages, key=lambda item: -item[0]):
             later(lag, tail, stage)
 
-        by_kind(now + 1, lambda: stage_hop(now + 1), None, None)
+        by_kind(now + 1, lambda: stage_hop(now + 1), lambda: stage_through_hop(now + 1))
 
         @pl.when((now >= 0) & (now < units))
         def _():

time: 115 us -> 114 us (level)
  no operation moved by 1% of the time
where the time goes in v6:
time: 114 us
  Pallas kernels  111 us (97%)
  local copies, waits for them, and re-layouts  2.29 us (2%)
    pallas_call x1, Pallas kernels, body(): pl.pallas_call(kernel, out_shape=jax.ShapeDtypeStruct((vectors, slots, sl...  111 us
    unnamed x1, local copies, waits for them, and re-layouts  2.29 us

profile of v6, /device:TPU:0, one launch (start us, length us, event | category | flops | bytes accessed | tf_op | source)
XLA Modules:
  0.0 113.6 jit_solution(2741308037872638348)
XLA Ops:
  0.0 111.3 %matvec.1 = bf16[2,8,64,512]{3,2,1,0:T(8,128)(2,1)} custom-call(s32[2]{0:T(128)} %shift_ref.1, s32[8]{0:T(128)} %dims_ref.1, bf16[2,8,512,512]{3,2,1,0:T(8,128)(2,1)} %wave_ref.1, bf16[2,8,4,2,64,512]{5,4,3,2,1,0:T(8,128)(2,1)} %bitcast.1, bf16[2,8,512,512]{3,2,1,0:T(8,128)(2,1)} %right_ref.1), custom_call_target="tpu_custom_call" | custom-call | tf_op jit(solution)/shard_map/matvec/pallas_call | solution.py:440
  111.3 2.3 %copy.7 = bf16[2,8,64,512]{3,2,1,0:T(8,128)(2,1)} copy(bf16[2,8,64,512]{3,2,1,0:T(8,128)(2,1)} %matvec.1) | data formatting | bytes 2097152

commit v7 on v6

--- a/solution.py
+++ b/solution.py
@@ -14,10 +14,10 @@
 DRAIN_LAG = max(LAGS + TAIL_LAGS) + 1
 RING = max(LAGS) + 1
 ENV_RING = 3
-BY_QUARTER = (3, 4, 10, 13)
-THROUGH_PAIR = (0, 1, 2, 5, 6)
-WHOLE = (12, 14, 15)
-Z_FIRST = (2, 8, 11, 14)
+BY_QUARTER = (0, 3, 4, 6, 10)
+THROUGH_PAIR = (1, 2, 7, 8)
+WHOLE = (11, 13, 15)
+Z_FIRST = (4, 8, 11, 14)
 Z_SLOTS = len(Z_FIRST)
 CHIP, SIDE, FWD_UP, FWD_DOWN, HOP_UP, HOP_DOWN, RELAY_UP, RELAY_DOWN, SUM_UP, SUM_DOWN = range(10)
 PAIR_FAR, PAIR_ABOVE, PAIR_BELOW, PAIR_OWN, FWD_PAIR = range(10, 15)

time: 114 us -> 112 us (0.982)
  Pallas kernels: 111 us -> 109 us
    pallas_call x1, Pallas kernels: 111 us -> 109 us  [body(): pl.pallas_call(kernel, out_shape=jax.ShapeDtypeStruct((vectors, slots, sl...]
where the time goes in v7:
time: 112 us
  Pallas kernels  109 us (97%)
  local copies, waits for them, and re-layouts  2.29 us (2%)
    pallas_call x1, Pallas kernels, body(): pl.pallas_call(kernel, out_shape=jax.ShapeDtypeStruct((vectors, slots, sl...  109 us
    unnamed x1, local copies, waits for them, and re-layouts  2.29 us

profile of v7, /device:TPU:0, one launch (start us, length us, event | category | flops | bytes accessed | tf_op | source)
XLA Modules:
  0.0 111.6 jit_solution(14592850573803969056)
XLA Ops:
  0.0 109.3 %matvec.1 = bf16[2,8,64,512]{3,2,1,0:T(8,128)(2,1)} custom-call(s32[2]{0:T(128)} %shift_ref.1, s32[8]{0:T(128)} %dims_ref.1, bf16[2,8,512,512]{3,2,1,0:T(8,128)(2,1)} %wave_ref.1, bf16[2,8,4,2,64,512]{5,4,3,2,1,0:T(8,128)(2,1)} %bitcast.1, bf16[2,8,512,512]{3,2,1,0:T(8,128)(2,1)} %right_ref.1), custom_call_target="tpu_custom_call" | custom-call | tf_op jit(solution)/shard_map/matvec/pallas_call | solution.py:440
  109.4 2.3 %copy.7 = bf16[2,8,64,512]{3,2,1,0:T(8,128)(2,1)} copy(bf16[2,8,64,512]{3,2,1,0:T(8,128)(2,1)} %matvec.1) | data formatting | bytes 2097152

commit v8 on v7

--- a/solution.py
+++ b/solution.py
@@ -14,10 +14,10 @@
 DRAIN_LAG = max(LAGS + TAIL_LAGS) + 1
 RING = max(LAGS) + 1
 ENV_RING = 3
-BY_QUARTER = (0, 3, 4, 6, 10)
-THROUGH_PAIR = (1, 2, 7, 8)
-WHOLE = (11, 13, 15)
-Z_FIRST = (4, 8, 11, 14)
+BY_QUARTER = (3, 4)
+THROUGH_PAIR = (0, 1, 2, 6, 7)
+WHOLE = (14, 15)
+Z_FIRST = (3, 7, 11, 14)
 Z_SLOTS = len(Z_FIRST)
 CHIP, SIDE, FWD_UP, FWD_DOWN, HOP_UP, HOP_DOWN, RELAY_UP, RELAY_DOWN, SUM_UP, SUM_DOWN = range(10)
 PAIR_FAR, PAIR_ABOVE, PAIR_BELOW, PAIR_OWN, FWD_PAIR = range(10, 15)

time: 112 us -> 112 us (level)
  no operation moved by 1% of the time
where the time goes in v8:
time: 112 us
  Pallas kernels  110 us (98%)
  local copies, waits for them, and re-layouts  2.29 us (2%)
    pallas_call x1, Pallas kernels, body(): pl.pallas_call(kernel, out_shape=jax.ShapeDtypeStruct((vectors, slots, sl...  110 us
    unnamed x1, local copies, waits for them, and re-layouts  2.29 us

profile of v8, /device:TPU:0, one launch (start us, length us, event | category | flops | bytes accessed | tf_op | source)
XLA Modules:
  0.0 111.8 jit_solution(1787504838393257412)
XLA Ops:
  0.0 109.5 %matvec.1 = bf16[2,8,64,512]{3,2,1,0:T(8,128)(2,1)} custom-call(s32[2]{0:T(128)} %shift_ref.1, s32[8]{0:T(128)} %dims_ref.1, bf16[2,8,512,512]{3,2,1,0:T(8,128)(2,1)} %wave_ref.1, bf16[2,8,4,2,64,512]{5,4,3,2,1,0:T(8,128)(2,1)} %bitcast.1, bf16[2,8,512,512]{3,2,1,0:T(8,128)(2,1)} %right_ref.1), custom_call_target="tpu_custom_call" | custom-call | tf_op jit(solution)/shard_map/matvec/pallas_call | solution.py:440
  109.5 2.3 %copy.7 = bf16[2,8,64,512]{3,2,1,0:T(8,128)(2,1)} copy(bf16[2,8,64,512]{3,2,1,0:T(8,128)(2,1)} %matvec.1) | data formatting | bytes 2097152
